TPU v7x, 256 devices: a whole 4x4x8 slice. The times are simulated.
256 devices in a mesh: row: 16 (over z, core), col: 16 (over y, x).
Axes of the slice: x: 4, y: 4, z: 8, core: 2. Of those that a mesh axis runs over, the one named last changes fastest.
Arguments:
- rhs: float32 [24576, 12288], P('row', 'col'), may hold values from -6 to 6
- panels_l: float32 [4, 24576, 512], P(None, 'row', 'col'), may hold values from -0.25 to 0.25
- diag_inverse: float32 [4, 512, 512], P(None, None, 'col'), may hold values from -1.5 to 1.5, as said below
Outputs:
- solved_rhs: float32 [24576, 12288], P('row', 'col')
Inputs may be any that keep to these rules, and one draw needn't show every extreme that they name: `diag_inverse`: each tile is lower triangular with diagonal entries between 0.5 and 1.5.
All inputs are finite; a program needn't handle non-finite values.
Results may differ from a plain program's by a relative error of at most 0.00016.
Values sent between devices are 32-bit elements; how exact they have to be, the bound alone decides.
A program may use at most 128 MiB of HBM per device.

v0:
```python
import jax
import jax.numpy as jnp
from jax import lax
from jax.sharding import PartitionSpec as P


def spread(x, axis, root):
    mine = lax.axis_index(axis) == root
    return lax.psum(jnp.where(mine, x, jnp.zeros_like(x)), axis)


def exact_dot(left, right):
    return jnp.dot(left, right, precision=lax.Precision.HIGHEST, preferred_element_type=jnp.float32)


def per_device(rhs, panels_l, diag_inverse):
    rows_here = rhs.shape[0]
    width = diag_inverse.shape[1]
    count = panels_l.shape[0]
    my_row = lax.axis_index("row")
    global_rows = my_row * rows_here + lax.iota(jnp.int32, rows_here)
    work = rhs
    for k in range(count):
        factor_cols = lax.all_gather(panels_l[k], "col", axis=1, tiled=True)
        inverse_tile = lax.all_gather(diag_inverse[k], "col", axis=1, tiled=True)
        owner = k * width // rows_here
        offset = k * width - owner * rows_here
        strip = work[offset : offset + width]
        is_owner = my_row == owner
        solved_here = lax.cond(
            is_owner,
            lambda: exact_dot(inverse_tile, strip),
            lambda: jnp.zeros(strip.shape, jnp.float32),
        )
        solved = spread(solved_here, "row", owner)
        update = exact_dot(factor_cols, solved)
        below = (global_rows >= (k + 1) * width)[:, None]
        work = jnp.where(below, work - update, work)
        work = work.at[offset : offset + width].set(
            jnp.where(is_owner, solved, work[offset : offset + width])
        )
    return work


def solution(mesh):
    in_specs = (P("row", "col"), P(None, "row", "col"), P(None, None, "col"))
    out_specs = P("row", "col")
    return jax.shard_map(
        per_device, mesh=mesh, in_specs=in_specs, out_specs=out_specs, check_vma=False
    )
```

profile of v0, /device:TPU:1, one launch (start us, length us, event | category | flops | bytes accessed | tf_op | source)
XLA Modules:
  0.0 919.6 jit_solution(2855108133627082533)
XLA Ops:
  6.5 1.0 fusion.27
  7.5 0.7 copy.52
  8.2 0.0 all-gather.17.cloned.1.call-update
  8.2 0.0 all-reduce.5.cloned.1.call-start
  8.3 51.0 %all-gather.17.cloned.1.call-done = f32[1,512,512]{1,0,2:T(1,128)} async-done(((f32[1,512,32]{1,0,2:T(1,128)}), f32[1,512,512]{1,0,2:T(1,128)}) %all-gather.17.cloned.1.call-update) | async-done | bytes 1048592 | tf_op jit(solution)/shard_map/all_gather | solution.py:25
  59.3 1.3 copy.69
  60.6 0.2 conditional.4
  60.6 0.2 broadcast.87.clone
  60.8 1.4 broadcast_select_fusion.3
  62.2 0.0 all-reduce.5.cloned.1.call-update
  62.2 0.0 all-gather.19.cloned.1.call-start
  62.2 1.1 copy-done.7
  63.3 0.9 fusion.26
  64.2 0.0 all-gather.19.cloned.1.call-update
  64.2 0.0 all-gather.21.cloned.1.call-start
  64.3 0.7 copy.53
  65.0 0.0 all-gather.21.cloned.1.call-update
  65.0 0.0 all-gather.23.cloned.1.call-start
  65.0 0.5 all-gather.23.cloned.1.call-update
  65.6 0.0 all-reduce.7.cloned.1.call-start
  65.6 6.0 copy.21
  71.7 105.5 %all-reduce.5.cloned.1.call-done = f32[512,768]{0,1:T(8,128)} async-done(((f32[512,768]{0,1:T(8,128)}), f32[512,768]{0,1:T(8,128)}) %all-reduce.5.cloned.1.call-update) | async-done | bytes 1572880 | tf_op jit(solution)/shard_map/psum | solution.py:9
  177.2 55.1 %all-gather.19.cloned.1.call-done = f32[1,1536,512]{1,2,0:T(8,128)} async-done(((f32[1,1536,32]{1,2,0:T(8,128)}), f32[1,1536,512]{1,2,0:T(8,128)}) %all-gather.19.cloned.1.call-update) | async-done | bytes 3145744 | tf_op jit(solution)/shard_map/all_gather | solution.py:24
  232.3 12.0 %subtract_select_fusion.3 = f32[1536,768]{0,1:T(8,128)} fusion(f32[1536,768]{0,1:T(8,128)} %copy.21, f32[512,768]{0,1:T(8,128)} %all-reduce.5.cloned.1.call-done, f32[1,1536,512]{1,2,0:T(8,128)} %all-gather.19.cloned.1.call-done, pred[1536]{0:T(1024)(128)(4,1)S(1)} %fusion.22), kind=kOutput, calls=%fused_computation.17 | convolution fusion | flops 7250116608 | bytes 14157312 | tf_op jit(solution)/shard_map/dot_general | solution.py:13
  244.3 2.9 fusion.21
  247.2 32.6 %all-gather.21.cloned.1.call-done = f32[1,512,512]{1,0,2:T(1,128)} async-done(((f32[1,512,32]{1,0,2:T(1,128)}), f32[1,512,512]{1,0,2:T(1,128)}) %all-gather.21.cloned.1.call-update) | async-done | bytes 1048592 | tf_op jit(solution)/shard_map/all_gather | solution.py:25
  279.8 0.4 conditional.5
  279.8 0.2 broadcast.88.clone
  280.2 1.3 broadcast_select_fusion.2
  281.5 0.0 all-reduce.7.cloned.1.call-update
  281.5 0.0 all-gather.25.cloned.1.call-start
  281.6 0.7 copy.54
  282.3 0.0 all-gather.27.cloned.1.call-start
  282.3 0.7 all-gather.27.cloned.1.call-update
  283.0 0.0 all-reduce.9.cloned.1.call-start
  283.1 52.3 %all-gather.23.cloned.1.call-done = f32[1,1536,512]{1,2,0:T(8,128)} async-done(((f32[1,1536,32]{1,2,0:T(8,128)}), f32[1,1536,512]{1,2,0:T(8,128)}) %all-gather.23.cloned.1.call-update) | async-done | bytes 3145744 | tf_op jit(solution)/shard_map/all_gather | solution.py:24
  335.5 115.4 %all-reduce.7.cloned.1.call-done = f32[512,768]{0,1:T(8,128)} async-done(((f32[512,768]{0,1:T(8,128)}), f32[512,768]{0,1:T(8,128)}) %all-reduce.7.cloned.1.call-update) | async-done | bytes 1572880 | tf_op jit(solution)/shard_map/psum | solution.py:9
  450.9 12.9 %subtract_select_fusion.2 = f32[1536,768]{0,1:T(8,128)} fusion(f32[1536,768]{0,1:T(8,128)} %fusion.21, f32[512,768]{0,1:T(8,128)} %all-reduce.7.cloned.1.call-done, f32[1,1536,512]{1,2,0:T(8,128)} %all-gather.23.cloned.1.call-done, pred[1536]{0:T(1024)(128)(4,1)S(1)} %fusion.23), kind=kOutput, calls=%fused_computation.16 | convolution fusion | flops 7250116608 | bytes 14157312 | tf_op jit(solution)/shard_map/dot_general | solution.py:13
  463.8 2.9 fusion.20
  466.7 32.8 %all-gather.25.cloned.1.call-done = f32[1,512,512]{1,0,2:T(1,128)} async-done(((f32[1,512,32]{1,0,2:T(1,128)}), f32[1,512,512]{1,0,2:T(1,128)}) %all-gather.25.cloned.1.call-update) | async-done | bytes 1048592 | tf_op jit(solution)/shard_map/all_gather | solution.py:25
  499.5 0.2 conditional.6
  499.5 0.2 broadcast.89.clone
  499.7 1.3 broadcast_select_fusion.1
  501.1 0.0 all-gather.29.cloned.1.call-start
  501.1 0.7 copy.55
  501.8 0.0 all-gather.29.cloned.1.call-update
  501.8 0.0 all-gather.31.cloned.1.call-start
  501.9 0.7 all-gather.31.cloned.1.call-update
  502.6 0.3 all-reduce.11.cloned.1.call-start
  502.8 52.5 %all-gather.27.cloned.1.call-done = f32[1,1536,512]{1,2,0:T(8,128)} async-done(((f32[1,1536,32]{1,2,0:T(8,128)}), f32[1,1536,512]{1,2,0:T(8,128)}) %all-gather.27.cloned.1.call-update) | async-done | bytes 3145744 | tf_op jit(solution)/shard_map/all_gather | solution.py:24
  555.3 115.6 %all-reduce.9.cloned.1.call-done = f32[512,768]{0,1:T(8,128)} async-done(((f32[512,768]{0,1:T(8,128)}), f32[512,768]{0,1:T(8,128)}) %all-reduce.9.cloned.1.call-update) | async-done | bytes 1572880 | tf_op jit(solution)/shard_map/psum | solution.py:9
  670.9 12.9 %subtract_select_fusion.1 = f32[1536,768]{0,1:T(8,128)} fusion(f32[1536,768]{0,1:T(8,128)} %fusion.20, f32[512,768]{0,1:T(8,128)} %all-reduce.9.cloned.1.call-done, f32[1,1536,512]{1,2,0:T(8,128)} %all-gather.27.cloned.1.call-done, pred[1536]{0:T(1024)(128)(4,1)S(1)} %fusion.24), kind=kOutput, calls=%fused_computation.15 | convolution fusion | flops 7250116608 | bytes 14157312 | tf_op jit(solution)/shard_map/dot_general | solution.py:13
  683.8 2.9 fusion.19
  686.7 32.7 %all-gather.29.cloned.1.call-done = f32[1,512,512]{1,0,2:T(1,128)} async-done(((f32[1,512,32]{1,0,2:T(1,128)}), f32[1,512,512]{1,0,2:T(1,128)}) %all-gather.29.cloned.1.call-update) | async-done | bytes 1048592 | tf_op jit(solution)/shard_map/all_gather | solution.py:25
  719.4 10.5 %conditional.7 = (f32[512,768]{0,1:T(8,128)S(1)}) conditional(s32[]{:T(128)} %convert_element_type.9, () %tuple.51, (f32[1536,768]{0,1:T(8,128)}, f32[1,512,512]{1,0,2:T(1,128)}) %tuple.52), branch_computations={%region_9.10_spmd, %region_10.11_spmd} | conditional | flops 2415919104 | bytes 17825828 | solution.py:30
  719.4 6.1 copy.32
  725.5 4.1 fusion.10
  729.8 1.3 broadcast_select_fusion
  731.2 0.0 all-reduce.11.cloned.1.call-update
  731.2 44.0 %all-gather.31.cloned.1.call-done = f32[1,1536,512]{1,2,0:T(8,128)} async-done(((f32[1,1536,32]{1,2,0:T(8,128)}), f32[1,1536,512]{1,2,0:T(8,128)}) %all-gather.31.cloned.1.call-update) | async-done | bytes 3145744 | tf_op jit(solution)/shard_map/all_gather | solution.py:24
  775.2 115.4 %all-reduce.11.cloned.1.call-done = f32[512,768]{0,1:T(8,128)} async-done(((f32[512,768]{0,1:T(8,128)}), f32[512,768]{0,1:T(8,128)}) %all-reduce.11.cloned.1.call-update) | async-done | bytes 1572880 | tf_op jit(solution)/shard_map/psum | solution.py:9
  890.6 13.1 %subtract_select_fusion = f32[1536,768]{0,1:T(8,128)} fusion(f32[1536,768]{0,1:T(8,128)} %fusion.19, f32[512,768]{0,1:T(8,128)} %all-reduce.11.cloned.1.call-done, f32[1,1536,512]{1,2,0:T(8,128)} %all-gather.31.cloned.1.call-done, pred[1536]{0:T(1024)(128)(4,1)S(1)} %fusion.25), kind=kOutput, calls=%fused_computation.14 | convolution fusion | flops 7250116608 | bytes 14157312 | tf_op jit(solution)/shard_map/dot_general | solution.py:13
  903.6 3.0 fusion.18
  906.7 6.0 copy.35
  (18 shorter events, 0.1 us)
Async XLA Ops:
  6.5 52.8 %all-gather.17.cloned.1.call-start = ((), (), s32[]{:S(2)}) async-start(), calls=%async_computation.4 | async-start | bytes 1114112 | tf_op jit(solution)/shard_map/all_gather | solution.py:25
  8.2 169.0 %all-reduce.5.cloned.1.call-start = ((), (), s32[]{:S(2)}) async-start(), calls=%async_computation | async-start | bytes 3145728 | tf_op jit(solution)/shard_map/psum | solution.py:9
  62.2 1.1 copy-start.7
  62.2 170.2 %all-gather.19.cloned.1.call-start = ((), (), s32[]{:S(2)}) async-start(), calls=%async_computation.5 | async-start | bytes 3342336 | tf_op jit(solution)/shard_map/all_gather | solution.py:24
  64.2 215.6 %all-gather.21.cloned.1.call-start = ((), (), s32[]{:S(2)}) async-start(), calls=%async_computation.6 | async-start | bytes 1114112 | tf_op jit(solution)/shard_map/all_gather | solution.py:25
  65.0 270.5 %all-gather.23.cloned.1.call-start = ((), (), s32[]{:S(2)}) async-start(), calls=%async_computation.7 | async-start | bytes 3342336 | tf_op jit(solution)/shard_map/all_gather | solution.py:24
  65.6 385.3 %all-reduce.7.cloned.1.call-start = ((), (), s32[]{:S(2)}) async-start(), calls=%async_computation.1 | async-start | bytes 3145728 | tf_op jit(solution)/shard_map/psum | solution.py:9
  177.2 67.1 %copy-start = (f32[512,768]{0,1:T(8,128)S(1)}, f32[512,768]{0,1:T(8,128)}, u32[]{:S(2)}) copy-start(f32[512,768]{0,1:T(8,128)} %all-reduce.5.cloned.1.call-done) | copy-start | bytes 4718596
  281.5 218.0 %all-gather.25.cloned.1.call-start = ((), (), s32[]{:S(2)}) async-start(), calls=%async_computation.8 | async-start | bytes 1114112 | tf_op jit(solution)/shard_map/all_gather | solution.py:25
  282.3 273.0 %all-gather.27.cloned.1.call-start = ((), (), s32[]{:S(2)}) async-start(), calls=%async_computation.9 | async-start | bytes 3342336 | tf_op jit(solution)/shard_map/all_gather | solution.py:24
  283.0 387.8 %all-reduce.9.cloned.1.call-start = ((), (), s32[]{:S(2)}) async-start(), calls=%async_computation.2 | async-start | bytes 3145728 | tf_op jit(solution)/shard_map/psum | solution.py:9
  450.9 12.9 %copy-start.2 = (f32[512,768]{0,1:T(8,128)S(1)}, f32[512,768]{0,1:T(8,128)}, u32[]{:S(2)}) copy-start(f32[512,768]{0,1:T(8,128)} %all-reduce.7.cloned.1.call-done) | copy-start | bytes 4718596
  501.1 218.3 %all-gather.29.cloned.1.call-start = ((), (), s32[]{:S(2)}) async-start(), calls=%async_computation.10 | async-start | bytes 1114112 | tf_op jit(solution)/shard_map/all_gather | solution.py:25
  501.8 273.4 %all-gather.31.cloned.1.call-start = ((), (), s32[]{:S(2)}) async-start(), calls=%async_computation.11 | async-start | bytes 3342336 | tf_op jit(solution)/shard_map/all_gather | solution.py:24
  502.6 388.0 %all-reduce.11.cloned.1.call-start = ((), (), s32[]{:S(2)}) async-start(), calls=%async_computation.3 | async-start | bytes 3145728 | tf_op jit(solution)/shard_map/psum | solution.py:9
  670.9 12.9 %copy-start.1 = (f32[512,768]{0,1:T(8,128)S(1)}, f32[512,768]{0,1:T(8,128)}, u32[]{:S(2)}) copy-start(f32[512,768]{0,1:T(8,128)} %all-reduce.9.cloned.1.call-done) | copy-start | bytes 4718596
  719.4 6.1 copy-start.4
  890.6 13.1 %copy-start.3 = (f32[512,768]{0,1:T(8,128)S(1)}, f32[512,768]{0,1:T(8,128)}, u32[]{:S(2)}) copy-start(f32[512,768]{0,1:T(8,128)} %all-reduce.11.cloned.1.call-done) | copy-start | bytes 4718596
Sparse Core Ops, SparseCore 0:
  9.8 49.4 all-gather.16
  62.3 114.8 all-reduce.4
  179.7 52.6 all-gather.18
  234.6 45.1 all-gather.20
  282.1 53.3 all-gather.22
  337.7 113.1 all-reduce.6
  453.3 46.1 all-gather.24
  501.9 53.3 all-gather.26
  557.7 113.1 all-reduce.8
  673.2 46.1 all-gather.28
  721.8 53.3 all-gather.30
  777.4 113.1 all-reduce.10
where the time goes:
time: 920 us
  waiting for transfers between devices  807 us (88%)
  matrix products  54.9 us (6%)
  local copies, waits for them, and re-layouts  25.7 us (3%)
  other arithmetic  17.1 us (2%)
  between operations  13.7 us (1%)
    psum x4, waiting for transfers between devices, spread(): return lax.psum(jnp.where(mine, x, jnp.zeros_like(x)), axis)  452 us
    all_gather x4, waiting for transfers between devices, per_device(): factor_cols = lax.all_gather(panels_l[k], 'col', axis=1, tiled=True)  204 us
    all_gather x4, waiting for transfers between devices, per_device(): inverse_tile = lax.all_gather(diag_inverse[k], 'col', axis=1, tiled=True)  149 us
    dot_general x4, matrix products, exact_dot(): jnp.dot(left, right, precision=lax.Precision.HIGHEST, preferred_element_t...  50.9 us
  transfers between devices with their start and end apart: 12, of which 12 were waited for; matrix products, arithmetic and copies ran while one was open for 8% of the time, Pallas kernels for 0%

commit v1 on v0

--- a/solution.py
+++ b/solution.py
@@ -22,7 +22,9 @@
     work = rhs
     for k in range(count):
         factor_cols = lax.all_gather(panels_l[k], "col", axis=1, tiled=True)
-        inverse_tile = lax.all_gather(diag_inverse[k], "col", axis=1, tiled=True)
+        inverse_tile = jnp.concatenate(
+            lax.all_to_all(jnp.stack([diag_inverse[k]] * lax.axis_size("col")), "col", 0, 0), axis=1
+        )
         owner = k * width // rows_here
         offset = k * width - owner * rows_here
         strip = work[offset : offset + width]

time: 920 us -> 594 us (0.65)
  waiting for transfers between devices: 807 us -> 454 us
  starting transfers between devices: 0.67 us -> 25.3 us
    all_gather x4, waiting for transfers between devices: 204 us -> 0.08 us  [per_device(): factor_cols = lax.all_gather(panels_l[k], 'col', axis=1, tiled=True)]
    all_gather x4 -> x0, waiting for transfers between devices: 149 us -> none  [per_device(): inverse_tile = lax.all_gather(diag_inverse[k], 'col', axis=1, tiled=True)]
    all_to_all x0 -> x4, starting transfers between devices: none -> 24.7 us  [per_device(): lax.all_to_all(jnp.stack([diag_inverse[k]] * lax.axis_size('col')), 'col'...]
    all_to_all x0 -> x4, waiting for transfers between devices: none -> 16 us  [per_device(): lax.all_to_all(jnp.stack([diag_inverse[k]] * lax.axis_size('col')), 'col'...]
    psum x4, waiting for transfers between devices: 452 us -> 436 us  [spread(): return lax.psum(jnp.where(mine, x, jnp.zeros_like(x)), axis)]
  transfers between devices with their start and end apart: 12 -> 12, of which waited for: 12 -> 5; matrix products, arithmetic and copies ran while one was open for 8% -> 12% of each run, Pallas kernels for 0% -> 0%
where the time goes in v1:
time: 594 us; the launch traced here: 593 us
  waiting for transfers between devices  454 us (76%)
  matrix products  55.3 us (9%)
  local copies, waits for them, and re-layouts  26 us (4%)
  starting transfers between devices  25.3 us (4%)
  other arithmetic  17 us (3%)
  between operations  15 us (3%)
    psum x4, waiting for transfers between devices, spread(): return lax.psum(jnp.where(mine, x, jnp.zeros_like(x)), axis)  436 us
    dot_general x4, matrix products, exact_dot(): jnp.dot(left, right, precision=lax.Precision.HIGHEST, preferred_element_t...  51.2 us
    all_to_all x4, starting transfers between devices, per_device(): lax.all_to_all(jnp.stack([diag_inverse[k]] * lax.axis_size('col')), 'col'...  24.7 us
    all_to_all x4, waiting for transfers between devices, per_device(): lax.all_to_all(jnp.stack([diag_inverse[k]] * lax.axis_size('col')), 'col'...  16 us
  transfers between devices with their start and end apart: 12, of which 5 were waited for; matrix products, arithmetic and copies ran while one was open for 12% of the time, Pallas kernels for 0%

profile of v1, /device:TPU:1, one launch (start us, length us, event | category | flops | bytes accessed | tf_op | source)
XLA Modules:
  0.0 593.0 jit_solution(14803463926284162298)
XLA Ops:
  7.4 1.0 slice_bitcast_fusion
  8.3 1.1 stack.12
  9.4 7.6 %all-to-all-start = ((f32[16,512,32]{1,2,0:T(8,128)}), f32[16,512,32]{1,2,0:T(8,128)S(1)}, u32[]{:S(2)}, u32[]{:S(2)}) async-start(f32[16,512,32]{1,2,0:T(8,128)} %stack.12), calls=%async_computation | async-start | bytes 2097152 | tf_op jit(solution)/shard_map/all_to_all | solution.py:26
  17.0 0.0 all-reduce.5.cloned.1.call-start
  17.1 16.0 %all-to-all-done = f32[16,512,32]{1,2,0:T(8,128)S(1)} async-done(((f32[16,512,32]{1,2,0:T(8,128)}), f32[16,512,32]{1,2,0:T(8,128)S(1)}, u32[]{:S(2)}, u32[]{:S(2)}) %all-to-all-start) | async-done | bytes 1048608 | tf_op jit(solution)/shard_map/all_to_all | solution.py:26
  33.0 0.2 conditional.4
  33.0 0.2 broadcast.91.clone
  33.2 1.4 broadcast_select_fusion.3
  34.6 0.0 all-reduce.5.cloned.1.call-update
  34.6 0.0 all-gather.9.cloned.1.call-start
  34.7 1.1 copy-done.4
  35.7 0.9 fusion.20
  36.6 0.0 all-gather.9.cloned.1.call-update
  36.7 0.0 all-gather.11.cloned.1.call-start
  36.7 0.5 all-gather.11.cloned.1.call-update
  37.3 1.1 stack.13
  38.3 4.2 all-to-all-start.1
  42.6 0.0 all-reduce.7.cloned.1.call-start
  42.6 6.1 %copy.19 = f32[1536,768]{0,1:T(8,128)} copy(f32[1536,768]{1,0:T(8,128)} %param.19) | data formatting | bytes 9437184 | tf_op args[0]
  48.7 102.0 %all-reduce.5.cloned.1.call-done = f32[512,768]{0,1:T(8,128)} async-done(((f32[512,768]{0,1:T(8,128)}), f32[512,768]{0,1:T(8,128)}) %all-reduce.5.cloned.1.call-update) | async-done | bytes 1572880 | tf_op jit(solution)/shard_map/psum | solution.py:9
  150.7 12.1 %subtract_select_fusion.3 = f32[1536,768]{0,1:T(8,128)} fusion(f32[1536,768]{0,1:T(8,128)} %copy.19, f32[512,768]{0,1:T(8,128)} %all-reduce.5.cloned.1.call-done, f32[1,1536,512]{1,2,0:T(8,128)} %all-gather.9.cloned.1.call-done, pred[1536]{0:T(1024)(128)(4,1)S(1)} %fusion.16), kind=kOutput, calls=%fused_computation.11 | convolution fusion | flops 7250116608 | bytes 14157312 | tf_op jit(solution)/shard_map/dot_general | solution.py:13
  162.8 0.0 copy-done
  162.8 2.9 fusion.15
  165.7 0.0 all-to-all-done.1
  165.7 0.4 conditional.5
  165.7 0.2 broadcast.92.clone
  166.0 1.3 broadcast_select_fusion.2
  167.3 0.0 all-reduce.7.cloned.1.call-update
  167.4 0.0 all-gather.13.cloned.1.call-start
  167.4 0.5 all-gather.13.cloned.1.call-update
  167.9 1.1 stack.14
  169.1 6.4 %all-to-all-start.2 = ((f32[16,512,32]{1,2,0:T(8,128)}), f32[16,512,32]{1,2,0:T(8,128)S(1)}, u32[]{:S(2)}, u32[]{:S(2)}) async-start(f32[16,512,32]{1,2,0:T(8,128)} %stack.14), calls=%async_computation.2 | async-start | bytes 2097152 | tf_op jit(solution)/shard_map/all_to_all | solution.py:26
  175.5 0.0 all-reduce.9.cloned.1.call-start
  175.5 0.0 all-gather.11.cloned.1.call-done
  175.6 112.6 %all-reduce.7.cloned.1.call-done = f32[512,768]{0,1:T(8,128)} async-done(((f32[512,768]{0,1:T(8,128)}), f32[512,768]{0,1:T(8,128)}) %all-reduce.7.cloned.1.call-update) | async-done | bytes 1572880 | tf_op jit(solution)/shard_map/psum | solution.py:9
  288.1 13.0 %subtract_select_fusion.2 = f32[1536,768]{0,1:T(8,128)} fusion(f32[1536,768]{0,1:T(8,128)} %fusion.15, f32[512,768]{0,1:T(8,128)} %all-reduce.7.cloned.1.call-done, f32[1,1536,512]{1,2,0:T(8,128)} %all-gather.11.cloned.1.call-done, pred[1536]{0:T(1024)(128)(4,1)S(1)} %fusion.17), kind=kOutput, calls=%fused_computation.10 | convolution fusion | flops 7250116608 | bytes 14157312 | tf_op jit(solution)/shard_map/dot_general | solution.py:13
  301.1 0.0 copy-done.2
  301.1 2.9 fusion.14
  304.0 0.0 all-to-all-done.2
  304.0 0.2 conditional.6
  304.0 0.2 broadcast.93.clone
  304.2 1.3 broadcast_select_fusion.1
  305.5 0.0 all-reduce.9.cloned.1.call-update
  305.5 0.0 all-gather.15.cloned.1.call-start
  305.6 0.7 all-gather.15.cloned.1.call-update
  306.3 1.1 stack.15
  307.4 6.5 %all-to-all-start.3 = ((f32[16,512,32]{1,2,0:T(8,128)}), f32[16,512,32]{1,2,0:T(8,128)S(1)}, u32[]{:S(2)}, u32[]{:S(2)}) async-start(f32[16,512,32]{1,2,0:T(8,128)} %stack.15), calls=%async_computation.3 | async-start | bytes 2097152 | tf_op jit(solution)/shard_map/all_to_all | solution.py:26
  313.9 0.3 all-reduce.11.cloned.1.call-start
  314.2 0.0 all-gather.13.cloned.1.call-done
  314.2 112.1 %all-reduce.9.cloned.1.call-done = f32[512,768]{0,1:T(8,128)} async-done(((f32[512,768]{0,1:T(8,128)}), f32[512,768]{0,1:T(8,128)}) %all-reduce.9.cloned.1.call-update) | async-done | bytes 1572880 | tf_op jit(solution)/shard_map/psum | solution.py:9
  426.4 13.0 %subtract_select_fusion.1 = f32[1536,768]{0,1:T(8,128)} fusion(f32[1536,768]{0,1:T(8,128)} %fusion.14, f32[512,768]{0,1:T(8,128)} %all-reduce.9.cloned.1.call-done, f32[1,1536,512]{1,2,0:T(8,128)} %all-gather.13.cloned.1.call-done, pred[1536]{0:T(1024)(128)(4,1)S(1)} %fusion.18), kind=kOutput, calls=%fused_computation.9 | convolution fusion | flops 7250116608 | bytes 14157312 | tf_op jit(solution)/shard_map/dot_general | solution.py:13
  439.4 0.0 copy-done.1
  439.4 2.9 fusion.13
  442.3 0.0 all-to-all-done.3
  442.3 10.4 %conditional.7 = (f32[512,768]{0,1:T(8,128)S(1)}) conditional(s32[]{:T(128)} %convert_element_type.9, () %tuple.51, (f32[512,16,32]{0,2,1:T(8,128)S(1)}, f32[1536,768]{0,1:T(8,128)}) %tuple.97), branch_computations={%region_9.10_spmd, %region_10.11_spmd} | conditional | flops 2415919104 | bytes 13631496 | solution.py:32
  442.3 6.1 %copy.25 = f32[1536,768]{1,0:T(8,128)} copy(f32[1536,768]{0,1:T(8,128)} %get-tuple-element.108) | data formatting | bytes 9437184 | tf_op jit(solution)/shard_map
  448.3 4.1 fusion.6
  452.7 1.3 broadcast_select_fusion
  454.0 0.0 all-reduce.11.cloned.1.call-update
  454.0 0.0 all-gather.15.cloned.1.call-done
  454.1 109.4 %all-reduce.11.cloned.1.call-done = f32[512,768]{0,1:T(8,128)} async-done(((f32[512,768]{0,1:T(8,128)}), f32[512,768]{0,1:T(8,128)}) %all-reduce.11.cloned.1.call-update) | async-done | bytes 1572880 | tf_op jit(solution)/shard_map/psum | solution.py:9
  563.5 13.1 %subtract_select_fusion = f32[1536,768]{0,1:T(8,128)} fusion(f32[1536,768]{0,1:T(8,128)} %fusion.13, f32[512,768]{0,1:T(8,128)} %all-reduce.11.cloned.1.call-done, f32[1,1536,512]{1,2,0:T(8,128)} %all-gather.15.cloned.1.call-done, pred[1536]{0:T(1024)(128)(4,1)S(1)} %fusion.19), kind=kOutput, calls=%fused_computation.8 | convolution fusion | flops 7250116608 | bytes 14157312 | tf_op jit(solution)/shard_map/dot_general | solution.py:13
  576.6 3.0 fusion.12
  579.6 6.0 %copy.27 = f32[1536,768]{1,0:T(8,128)} copy(f32[1536,768]{0,1:T(8,128)} %fusion.12) | data formatting | bytes 9437184 | tf_op jit(solution)/shard_map/scatter | solution.py:41
  (11 shorter events, 0.0 us)
Async XLA Ops:
  9.4 23.6 %all-to-all-start = ((f32[16,512,32]{1,2,0:T(8,128)}), f32[16,512,32]{1,2,0:T(8,128)S(1)}, u32[]{:S(2)}, u32[]{:S(2)}) async-start(f32[16,512,32]{1,2,0:T(8,128)} %stack.12), calls=%async_computation | async-start | bytes 2097152 | tf_op jit(solution)/shard_map/all_to_all | solution.py:26
  17.0 133.7 %all-reduce.5.cloned.1.call-start = ((), (), s32[]{:S(2)}) async-start(), calls=%async_computation.4 | async-start | bytes 3145728 | tf_op jit(solution)/shard_map/psum | solution.py:9
  34.6 1.1 copy-start.4
  34.6 116.0 %all-gather.9.cloned.1.call-start = ((), (), s32[]{:S(2)}) async-start(), calls=%async_computation.8 | async-start | bytes 3342336 | tf_op jit(solution)/shard_map/all_gather | solution.py:24
  36.7 138.9 %all-gather.11.cloned.1.call-start = ((), (), s32[]{:S(2)}) async-start(), calls=%async_computation.9 | async-start | bytes 3342336 | tf_op jit(solution)/shard_map/all_gather | solution.py:24
  38.3 127.3 %all-to-all-start.1 = ((f32[16,512,32]{1,2,0:T(8,128)}), f32[16,512,32]{1,2,0:T(8,128)S(1)}, u32[]{:S(2)}, u32[]{:S(2)}) async-start(f32[16,512,32]{1,2,0:T(8,128)} %stack.13), calls=%async_computation.1 | async-start | bytes 2097152 | tf_op jit(solution)/shard_map/all_to_all | solution.py:26
  42.6 245.6 %all-reduce.7.cloned.1.call-start = ((), (), s32[]{:S(2)}) async-start(), calls=%async_computation.5 | async-start | bytes 3145728 | tf_op jit(solution)/shard_map/psum | solution.py:9
  150.7 12.1 %copy-start = (f32[512,768]{0,1:T(8,128)S(1)}, f32[512,768]{0,1:T(8,128)}, u32[]{:S(2)}) copy-start(f32[512,768]{0,1:T(8,128)} %all-reduce.5.cloned.1.call-done) | copy-start | bytes 4718596
  167.4 146.9 %all-gather.13.cloned.1.call-start = ((), (), s32[]{:S(2)}) async-start(), calls=%async_computation.10 | async-start | bytes 3342336 | tf_op jit(solution)/shard_map/all_gather | solution.py:24
  169.1 134.9 %all-to-all-start.2 = ((f32[16,512,32]{1,2,0:T(8,128)}), f32[16,512,32]{1,2,0:T(8,128)S(1)}, u32[]{:S(2)}, u32[]{:S(2)}) async-start(f32[16,512,32]{1,2,0:T(8,128)} %stack.14), calls=%async_computation.2 | async-start | bytes 2097152 | tf_op jit(solution)/shard_map/all_to_all | solution.py:26
  175.5 250.9 %all-reduce.9.cloned.1.call-start = ((), (), s32[]{:S(2)}) async-start(), calls=%async_computation.6 | async-start | bytes 3145728 | tf_op jit(solution)/shard_map/psum | solution.py:9
  288.1 13.0 %copy-start.2 = (f32[512,768]{0,1:T(8,128)S(1)}, f32[512,768]{0,1:T(8,128)}, u32[]{:S(2)}) copy-start(f32[512,768]{0,1:T(8,128)} %all-reduce.7.cloned.1.call-done) | copy-start | bytes 4718596
  305.5 148.5 %all-gather.15.cloned.1.call-start = ((), (), s32[]{:S(2)}) async-start(), calls=%async_computation.11 | async-start | bytes 3342336 | tf_op jit(solution)/shard_map/all_gather | solution.py:24
  307.4 134.9 %all-to-all-start.3 = ((f32[16,512,32]{1,2,0:T(8,128)}), f32[16,512,32]{1,2,0:T(8,128)S(1)}, u32[]{:S(2)}, u32[]{:S(2)}) async-start(f32[16,512,32]{1,2,0:T(8,128)} %stack.15), calls=%async_computation.3 | async-start | bytes 2097152 | tf_op jit(solution)/shard_map/all_to_all | solution.py:26
  313.9 249.6 %all-reduce.11.cloned.1.call-start = ((), (), s32[]{:S(2)}) async-start(), calls=%async_computation.7 | async-start | bytes 3145728 | tf_op jit(solution)/shard_map/psum | solution.py:9
  426.4 13.0 %copy-start.1 = (f32[512,768]{0,1:T(8,128)S(1)}, f32[512,768]{0,1:T(8,128)}, u32[]{:S(2)}) copy-start(f32[512,768]{0,1:T(8,128)} %all-reduce.9.cloned.1.call-done) | copy-start | bytes 4718596
  563.5 13.1 %copy-start.3 = (f32[512,768]{0,1:T(8,128)S(1)}, f32[512,768]{0,1:T(8,128)}, u32[]{:S(2)}) copy-start(f32[512,768]{0,1:T(8,128)} %all-reduce.11.cloned.1.call-done) | copy-start | bytes 4718596
Sparse Core Ops, SparseCore 0:
  34.7 115.8 all-reduce.4
  167.5 120.5 all-reduce.6
  305.7 120.6 all-reduce.8
  454.1 109.2 all-reduce.10
Sparse Core Ops, SparseCore 1:
  37.5 57.0 all-gather.8
  96.9 51.5 all-gather.10
  170.3 57.9 all-gather.12
  308.8 58.1 all-gather.14
